TPU v7x, 256 devices: a whole 4x4x8 slice. The times are simulated.
256 devices in a mesh: row: 32 (over y, z), col: 8 (over x, core).
Axes of the slice: x: 4, y: 4, z: 8, core: 2. Of those that a mesh axis runs over, the one named last changes fastest.
Arguments:
- acts: bfloat16 [6144, 28672], P('col', 'row'), may hold values from -12 to 12
- out_grad: bfloat16 [6144, 8192], P('row', 'col'), may hold values from -12 to 12
- lengths: int32 [8], replicated, may hold values from 1 to 768, 4800 in all
Outputs:
- weight_grad: bfloat16 [28672, 8192], P('row', 'col')
- norms: float32 [8], replicated
All inputs are finite; a program needn't handle non-finite values.
Results may differ from a plain program's by a relative error of at most 0.0013.
Values may be sent and summed in bfloat16 or wider, within the bound.
No kernel may reach another device: no remote copies, remote signals or barrier semaphores. Data moves between devices by JAX's collectives and lax.ppermute only.
A program may use at most 128 MiB of HBM per device.

v0:
```python
import jax
import jax.numpy as jnp
from jax import lax
from jax.sharding import PartitionSpec as P

FF = 28672
D = 8192


def body(acts, out_grad, lengths):
    n_row = lax.axis_size("row")
    own_rows = out_grad.shape[0]
    tokens = own_rows * n_row
    seqs = lengths.shape[0]
    seq_len = tokens // seqs
    slot = lax.broadcasted_iota(jnp.int32, (seq_len, 1), 0)
    act_full = lax.all_gather(acts, "col", axis=0, tiled=True)
    grad_full = lax.all_gather(out_grad, "row", axis=0, tiled=True)
    products = []
    locals_ = []
    for seq in range(seqs):
        act_rows = act_full[seq * seq_len : (seq + 1) * seq_len]
        grad_rows = grad_full[seq * seq_len : (seq + 1) * seq_len]
        grad_rows = jnp.where(slot < lengths[seq], grad_rows, jnp.zeros_like(grad_rows))
        product = lax.dot_general(
            act_rows, grad_rows, (((0,), (0,)), ((), ())), preferred_element_type=jnp.float32
        )
        products.append(product)
        locals_.append(jnp.sum(product * product))
    squares = lax.psum(jnp.stack(locals_), ("row", "col"))
    divisor = float(FF) * float(D) * float(seq_len)
    norms = jnp.sqrt(squares / divisor)
    scale = 1.0 / (norms + 0.1)
    total = scale[0] * products[0]
    for seq in range(1, seqs):
        total = total + scale[seq] * products[seq]
    weight_grad = (total / jnp.sqrt(jnp.float32(tokens))).astype(jnp.bfloat16)
    return (weight_grad, norms)


def solution(mesh):
    placed = (P("col", "row"), P("row", "col"), P())
    return jax.shard_map(
        body, mesh=mesh, in_specs=placed, out_specs=(P("row", "col"), P()), check_vma=False
    )
```

profile of v0, /device:TPU:1, one launch (start us, length us, event | category | flops | bytes accessed | tf_op | source)
XLA Modules:
  0.0 344.8 jit_solution(8986895510977710011)
XLA Ops:
  7.2 0.7 all-gather.5.cloned.1.call-update
  7.9 0.7 all-gather.3.cloned.1.call-update
  8.6 1.6 fusion.42
  10.3 0.7 iota_compare_fusion.1
  10.9 0.7 iota_compare_fusion.2
  12.2 0.7 iota_compare_fusion.4
  12.9 0.6 iota_compare_fusion.5
  13.5 0.6 iota_compare_fusion.6
  14.1 0.6 iota_compare_fusion.7
  15.3 62.0 %all-gather.5.cloned.1.call-done = bf16[6144,896]{1,0:T(8,128)(2,1)} async-done(((bf16[768,896]{1,0:T(8,128)(2,1)}), bf16[6144,896]{1,0:T(8,128)(2,1)}) %all-gather.5.cloned.1.call-update) | async-done | bytes 11010064 | tf_op jit(solution)/shard_map/all_gather | solution.py:17
  77.3 121.9 %all-gather.3.cloned.1.call-done = bf16[6144,1024]{1,0:T(8,128)(2,1)} async-done(((bf16[192,1024]{1,0:T(8,128)(2,1)}), bf16[6144,1024]{1,0:T(8,128)(2,1)}) %all-gather.3.cloned.1.call-update) | async-done | bytes 12582928 | tf_op jit(solution)/shard_map/all_gather | solution.py:18
  199.2 6.4 %multiply_reduce_fusion = (f32[]{:T(128)}, f32[1024,896]{1,0:T(8,128)}) fusion(bf16[6144,896]{1,0:T(8,128)(2,1)} %all-gather.5.cloned.1.call-done, bf16[6144,1024]{1,0:T(8,128)(2,1)} %all-gather.3.cloned.1.call-done, pred[768]{0:T(1024)(128)(4,1)S(1)} %iota_compare_fusion), kind=kOutput, calls=%fused_computation.1 | convolution fusion | flops 1411907584 | bytes 6619908 | tf_op jit(solution)/shard_map/dot_general | solution.py:25
  206.0 5.9 %multiply_reduce_fusion.7 = (f32[]{:T(128)}, f32[1024,896]{1,0:T(8,128)}) fusion(bf16[6144,896]{1,0:T(8,128)(2,1)} %all-gather.5.cloned.1.call-done, bf16[6144,1024]{1,0:T(8,128)(2,1)S(1)} %copy-done, pred[768]{0:T(1024)(128)(4,1)S(1)} %iota_compare_fusion.7), kind=kOutput, calls=%fused_computation.8 | convolution fusion | flops 1411907584 | bytes 6620164 | tf_op jit(solution)/shard_map/dot_general | solution.py:25
  211.8 4.5 %multiply_reduce_fusion.6 = (f32[]{:T(128)}, f32[1024,896]{1,0:T(8,128)}) fusion(bf16[6144,896]{1,0:T(8,128)(2,1)S(1)} %copy-done.1, bf16[6144,1024]{1,0:T(8,128)(2,1)S(1)} %copy-done, pred[768]{0:T(1024)(128)(4,1)S(1)} %iota_compare_fusion.6), kind=kOutput, calls=%fused_computation.7 | convolution fusion | flops 1411907584 | bytes 6620164 | tf_op jit(solution)/shard_map/dot_general | solution.py:25
  216.3 4.5 %multiply_reduce_fusion.5 = (f32[]{:T(128)}, f32[1024,896]{1,0:T(8,128)}) fusion(bf16[6144,896]{1,0:T(8,128)(2,1)S(1)} %copy-done.1, bf16[6144,1024]{1,0:T(8,128)(2,1)S(1)} %copy-done, pred[768]{0:T(1024)(128)(4,1)S(1)} %iota_compare_fusion.5), kind=kOutput, calls=%fused_computation.6 | convolution fusion | flops 1411907584 | bytes 6620164 | tf_op jit(solution)/shard_map/dot_general | solution.py:25
  220.8 4.5 %multiply_reduce_fusion.4 = (f32[]{:T(128)}, f32[1024,896]{1,0:T(8,128)}) fusion(bf16[6144,896]{1,0:T(8,128)(2,1)S(1)} %copy-done.1, bf16[6144,1024]{1,0:T(8,128)(2,1)S(1)} %copy-done, pred[768]{0:T(1024)(128)(4,1)S(1)} %iota_compare_fusion.4), kind=kOutput, calls=%fused_computation.5 | convolution fusion | flops 1411907584 | bytes 6620164 | tf_op jit(solution)/shard_map/dot_general | solution.py:25
  225.3 4.4 %multiply_reduce_fusion.3 = (f32[]{:T(128)}, f32[1024,896]{1,0:T(8,128)}) fusion(bf16[6144,896]{1,0:T(8,128)(2,1)S(1)} %copy-done.1, bf16[6144,1024]{1,0:T(8,128)(2,1)S(1)} %copy-done, pred[768]{0:T(1024)(128)(4,1)S(1)} %iota_compare_fusion.3), kind=kOutput, calls=%fused_computation.4 | convolution fusion | flops 1411907584 | bytes 6620164 | tf_op jit(solution)/shard_map/dot_general | solution.py:25
  229.8 4.6 %multiply_reduce_fusion.2 = (f32[]{:T(128)}, f32[1024,896]{1,0:T(8,128)}) fusion(bf16[6144,896]{1,0:T(8,128)(2,1)S(1)} %copy-done.1, bf16[6144,1024]{1,0:T(8,128)(2,1)S(1)} %copy-done, pred[768]{0:T(1024)(128)(4,1)S(1)} %iota_compare_fusion.2), kind=kOutput, calls=%fused_computation.3 | convolution fusion | flops 1411907584 | bytes 6620164 | tf_op jit(solution)/shard_map/dot_general | solution.py:25
  234.4 4.5 %multiply_reduce_fusion.1 = (f32[]{:T(128)}, f32[1024,896]{1,0:T(8,128)}) fusion(bf16[6144,896]{1,0:T(8,128)(2,1)S(1)} %copy-done.1, bf16[6144,1024]{1,0:T(8,128)(2,1)S(1)} %copy-done, pred[768]{0:T(1024)(128)(4,1)S(1)} %iota_compare_fusion.1), kind=kOutput, calls=%fused_computation.2 | convolution fusion | flops 1411907584 | bytes 6620164 | tf_op jit(solution)/shard_map/dot_general | solution.py:25
  238.9 5.1 %stack.35 = f32[8]{0:T(128)S(1)} concatenate(f32[1]{0:T(128)} %bitcast.1, f32[1]{0:T(128)} %bitcast.3, f32[1]{0:T(128)} %bitcast.5, f32[1]{0:T(128)} %bitcast.7, f32[1]{0:T(128)} %bitcast.9, f32[1]{0:T(128)} %bitcast.11, f32[1]{0:T(128)} %bitcast.13, f32[1]{0:T(128)} %bitcast.15), dimensions={0} | concatenate | bytes 64 | tf_op jit(solution)/shard_map/stack | solution.py:30
  244.0 74.9 %psum.7 = f32[8]{0:T(128)S(1)} all-reduce(f32[8]{0:T(128)S(1)} %stack.35), channel_id=1, replica_groups=mesh['row'=32,'col'=8] {'row','col'}, use_global_device_ids=true, to_apply=%region_8.9 | all-reduce | flops 8 | bytes 64 | tf_op jit(solution)/shard_map/psum | solution.py:30
  319.5 0.7 fusion.41
  320.1 15.4 %fusion = bf16[896,1024]{0,1:T(8,128)(2,1)S(1)} fusion(f32[1024,896]{1,0:T(8,128)} %get-tuple-element.37, f32[]{:T(128)} %bitcast.23, f32[1024,896]{1,0:T(8,128)} %get-tuple-element.35, f32[]{:T(128)} %bitcast.22, f32[1024,896]{1,0:T(8,128)} %get-tuple-element.33, f32[]{:T(128)} %bitcast.21, f32[1024,896]{1,0:T(8,128)} %get-tuple-element.31, f32[]{:T(128)} %bitcast.20, ...), kind=kLoop, calls=%fused_computation.9 | loop fusion | flops 15597568 | bytes 31195168 | tf_op jit(solution)/shard_map/convert_element_type | solution.py:37
  335.6 2.4 copy.5
  (9 shorter events, 2.2 us)
Async XLA Ops:
  7.2 70.2 %all-gather.5.cloned.1.call-start = ((), (), s32[]{:S(2)}) async-start(), calls=%async_computation.1 | async-start | bytes 12386304 | tf_op jit(solution)/shard_map/all_gather | solution.py:17
  7.9 191.3 %all-gather.3.cloned.1.call-start = ((), (), s32[]{:S(2)}) async-start(), calls=%async_computation | async-start | bytes 12976128 | tf_op jit(solution)/shard_map/all_gather | solution.py:18
  199.2 6.8 %copy-start = (bf16[6144,1024]{1,0:T(8,128)(2,1)S(1)}, bf16[6144,1024]{1,0:T(8,128)(2,1)}, u32[]{:S(2)}) copy-start(bf16[6144,1024]{1,0:T(8,128)(2,1)} %all-gather.3.cloned.1.call-done) | copy-start | bytes 37748740
  206.0 5.9 %copy-start.1 = (bf16[6144,896]{1,0:T(8,128)(2,1)S(1)}, bf16[6144,896]{1,0:T(8,128)(2,1)}, u32[]{:S(2)}) copy-start(bf16[6144,896]{1,0:T(8,128)(2,1)} %all-gather.5.cloned.1.call-done) | copy-start | bytes 33030148
Sparse Core Ops, SparseCore 0:
  9.8 67.4 all-gather.4
  79.9 119.2 all-gather.2
where the time goes:
time: 345 us
  waiting for transfers between devices  185 us (54%)
  blocking collectives  74.9 us (22%)
  matrix products  39.3 us (11%)
  other arithmetic  20.9 us (6%)
  between operations  14.1 us (4%)
  local copies, waits for them, and re-layouts  10.2 us (3%)
    all_gather x1, waiting for transfers between devices, body(): grad_full = lax.all_gather(out_grad, 'row', axis=0, tiled=True)  122 us
    psum x1, blocking collectives, body(): squares = lax.psum(jnp.stack(locals_), ('row', 'col'))  74.9 us
    all_gather x1, waiting for transfers between devices, body(): act_full = lax.all_gather(acts, 'col', axis=0, tiled=True)  62 us
    dot_general x8, matrix products, body(): lax.dot_general(act_rows, grad_rows, (((0,), (0,)), ((), ())), preferred_...  39.3 us
    convert_element_type x1, other arithmetic, body(): weight_grad = (total / jnp.sqrt(jnp.float32(tokens))).astype(jnp.bfloat16)  15.4 us
  transfers between devices with their start and end apart: 2, of which 2 were waited for; matrix products, arithmetic and copies ran while one was open for 2% of the time, Pallas kernels for 0%

commit v1 on v0

--- a/solution.py
+++ b/solution.py
@@ -27,7 +27,7 @@
         )
         products.append(product)
         locals_.append(jnp.sum(product * product))
-    squares = lax.psum(jnp.stack(locals_), ("row", "col"))
+    squares = lax.psum(lax.psum(jnp.stack(locals_), "row"), "col")
     divisor = float(FF) * float(D) * float(seq_len)
     norms = jnp.sqrt(squares / divisor)
     scale = 1.0 / (norms + 0.1)

time: 345 us -> 354 us (1.026)
  blocking collectives: 74.9 us -> 84 us
    psum x1 -> x2, blocking collectives: 74.9 us -> 84 us  [body(): squares = lax.psum(lax.psum(jnp.stack(locals_), 'row'), 'col')]
where the time goes in v1:
time: 354 us
  waiting for transfers between devices  185 us (52%)
  blocking collectives  84 us (24%)
  matrix products  39.3 us (11%)
  other arithmetic  20.9 us (6%)
  between operations  14.1 us (4%)
  local copies, waits for them, and re-layouts  10.2 us (3%)
    all_gather x1, waiting for transfers between devices, body(): grad_full = lax.all_gather(out_grad, 'row', axis=0, tiled=True)  122 us
    psum x2, blocking collectives, body(): squares = lax.psum(lax.psum(jnp.stack(locals_), 'row'), 'col')  84 us
    all_gather x1, waiting for transfers between devices, body(): act_full = lax.all_gather(acts, 'col', axis=0, tiled=True)  62 us
    dot_general x8, matrix products, body(): lax.dot_general(act_rows, grad_rows, (((0,), (0,)), ((), ())), preferred_...  39.3 us
    convert_element_type x1, other arithmetic, body(): weight_grad = (total / jnp.sqrt(jnp.float32(tokens))).astype(jnp.bfloat16)  15.4 us
  transfers between devices with their start and end apart: 2, of which 2 were waited for; matrix products, arithmetic and copies ran while one was open for 2% of the time, Pallas kernels for 0%

profile of v1, /device:TPU:1, one launch (start us, length us, event | category | flops | bytes accessed | tf_op | source)
XLA Modules:
  0.0 353.9 jit_solution(7848185008573694140)
XLA Ops:
  7.2 0.7 all-gather.5.cloned.1.call-update
  7.9 0.7 all-gather.3.cloned.1.call-update
  8.6 1.6 fusion.42
  10.3 0.7 iota_compare_fusion.1
  10.9 0.7 iota_compare_fusion.2
  12.2 0.7 iota_compare_fusion.4
  12.9 0.6 iota_compare_fusion.5
  13.5 0.6 iota_compare_fusion.6
  15.3 62.0 %all-gather.5.cloned.1.call-done = bf16[6144,896]{1,0:T(8,128)(2,1)} async-done(((bf16[768,896]{1,0:T(8,128)(2,1)}), bf16[6144,896]{1,0:T(8,128)(2,1)}) %all-gather.5.cloned.1.call-update) | async-done | bytes 11010064 | tf_op jit(solution)/shard_map/all_gather | solution.py:17
  77.3 121.9 %all-gather.3.cloned.1.call-done = bf16[6144,1024]{1,0:T(8,128)(2,1)} async-done(((bf16[192,1024]{1,0:T(8,128)(2,1)}), bf16[6144,1024]{1,0:T(8,128)(2,1)}) %all-gather.3.cloned.1.call-update) | async-done | bytes 12582928 | tf_op jit(solution)/shard_map/all_gather | solution.py:18
  199.2 6.4 %multiply_reduce_fusion = (f32[]{:T(128)}, f32[1024,896]{1,0:T(8,128)}) fusion(bf16[6144,896]{1,0:T(8,128)(2,1)} %all-gather.5.cloned.1.call-done, bf16[6144,1024]{1,0:T(8,128)(2,1)} %all-gather.3.cloned.1.call-done, pred[768]{0:T(1024)(128)(4,1)S(1)} %iota_compare_fusion), kind=kOutput, calls=%fused_computation.1 | convolution fusion | flops 1411907584 | bytes 6619908 | tf_op jit(solution)/shard_map/dot_general | solution.py:25
  206.0 5.9 %multiply_reduce_fusion.7 = (f32[]{:T(128)}, f32[1024,896]{1,0:T(8,128)}) fusion(bf16[6144,896]{1,0:T(8,128)(2,1)} %all-gather.5.cloned.1.call-done, bf16[6144,1024]{1,0:T(8,128)(2,1)S(1)} %copy-done, pred[768]{0:T(1024)(128)(4,1)S(1)} %iota_compare_fusion.7), kind=kOutput, calls=%fused_computation.8 | convolution fusion | flops 1411907584 | bytes 6620164 | tf_op jit(solution)/shard_map/dot_general | solution.py:25
  211.8 4.5 %multiply_reduce_fusion.6 = (f32[]{:T(128)}, f32[1024,896]{1,0:T(8,128)}) fusion(bf16[6144,896]{1,0:T(8,128)(2,1)S(1)} %copy-done.1, bf16[6144,1024]{1,0:T(8,128)(2,1)S(1)} %copy-done, pred[768]{0:T(1024)(128)(4,1)S(1)} %iota_compare_fusion.6), kind=kOutput, calls=%fused_computation.7 | convolution fusion | flops 1411907584 | bytes 6620164 | tf_op jit(solution)/shard_map/dot_general | solution.py:25
  216.3 4.5 %multiply_reduce_fusion.5 = (f32[]{:T(128)}, f32[1024,896]{1,0:T(8,128)}) fusion(bf16[6144,896]{1,0:T(8,128)(2,1)S(1)} %copy-done.1, bf16[6144,1024]{1,0:T(8,128)(2,1)S(1)} %copy-done, pred[768]{0:T(1024)(128)(4,1)S(1)} %iota_compare_fusion.5), kind=kOutput, calls=%fused_computation.6 | convolution fusion | flops 1411907584 | bytes 6620164 | tf_op jit(solution)/shard_map/dot_general | solution.py:25
  220.8 4.5 %multiply_reduce_fusion.4 = (f32[]{:T(128)}, f32[1024,896]{1,0:T(8,128)}) fusion(bf16[6144,896]{1,0:T(8,128)(2,1)S(1)} %copy-done.1, bf16[6144,1024]{1,0:T(8,128)(2,1)S(1)} %copy-done, pred[768]{0:T(1024)(128)(4,1)S(1)} %iota_compare_fusion.4), kind=kOutput, calls=%fused_computation.5 | convolution fusion | flops 1411907584 | bytes 6620164 | tf_op jit(solution)/shard_map/dot_general | solution.py:25
  225.3 4.4 %multiply_reduce_fusion.3 = (f32[]{:T(128)}, f32[1024,896]{1,0:T(8,128)}) fusion(bf16[6144,896]{1,0:T(8,128)(2,1)S(1)} %copy-done.1, bf16[6144,1024]{1,0:T(8,128)(2,1)S(1)} %copy-done, pred[768]{0:T(1024)(128)(4,1)S(1)} %iota_compare_fusion.3), kind=kOutput, calls=%fused_computation.4 | convolution fusion | flops 1411907584 | bytes 6620164 | tf_op jit(solution)/shard_map/dot_general | solution.py:25
  229.8 4.6 %multiply_reduce_fusion.2 = (f32[]{:T(128)}, f32[1024,896]{1,0:T(8,128)}) fusion(bf16[6144,896]{1,0:T(8,128)(2,1)S(1)} %copy-done.1, bf16[6144,1024]{1,0:T(8,128)(2,1)S(1)} %copy-done, pred[768]{0:T(1024)(128)(4,1)S(1)} %iota_compare_fusion.2), kind=kOutput, calls=%fused_computation.3 | convolution fusion | flops 1411907584 | bytes 6620164 | tf_op jit(solution)/shard_map/dot_general | solution.py:25
  234.4 4.5 %multiply_reduce_fusion.1 = (f32[]{:T(128)}, f32[1024,896]{1,0:T(8,128)}) fusion(bf16[6144,896]{1,0:T(8,128)(2,1)S(1)} %copy-done.1, bf16[6144,1024]{1,0:T(8,128)(2,1)S(1)} %copy-done, pred[768]{0:T(1024)(128)(4,1)S(1)} %iota_compare_fusion.1), kind=kOutput, calls=%fused_computation.2 | convolution fusion | flops 1411907584 | bytes 6620164 | tf_op jit(solution)/shard_map/dot_general | solution.py:25
  238.9 5.1 %stack.35 = f32[8]{0:T(128)S(1)} concatenate(f32[1]{0:T(128)} %bitcast.1, f32[1]{0:T(128)} %bitcast.3, f32[1]{0:T(128)} %bitcast.5, f32[1]{0:T(128)} %bitcast.7, f32[1]{0:T(128)} %bitcast.9, f32[1]{0:T(128)} %bitcast.11, f32[1]{0:T(128)} %bitcast.13, f32[1]{0:T(128)} %bitcast.15), dimensions={0} | concatenate | bytes 64 | tf_op jit(solution)/shard_map/stack | solution.py:30
  244.0 57.6 %psum.14 = f32[8]{0:T(128)S(1)} all-reduce(f32[8]{0:T(128)S(1)} %stack.35), channel_id=1, replica_groups=mesh['row'=32,'col'=8] {'row'}, use_global_device_ids=true, to_apply=%region_8.9 | all-reduce | flops 8 | bytes 64 | tf_op jit(solution)/shard_map/psum | solution.py:30
  301.6 26.4 %psum.15 = f32[8]{0:T(128)S(1)} all-reduce(f32[8]{0:T(128)S(1)} %psum.14), channel_id=1, replica_groups=mesh['row'=32,'col'=8] {'col'}, use_global_device_ids=true, to_apply=%region_9.10 | all-reduce | flops 8 | bytes 64 | tf_op jit(solution)/shard_map/psum | solution.py:30
  328.6 0.7 fusion.41
  329.2 15.4 %fusion = bf16[896,1024]{0,1:T(8,128)(2,1)S(1)} fusion(f32[1024,896]{1,0:T(8,128)} %get-tuple-element.37, f32[]{:T(128)} %bitcast.23, f32[1024,896]{1,0:T(8,128)} %get-tuple-element.35, f32[]{:T(128)} %bitcast.22, f32[1024,896]{1,0:T(8,128)} %get-tuple-element.33, f32[]{:T(128)} %bitcast.21, f32[1024,896]{1,0:T(8,128)} %get-tuple-element.31, f32[]{:T(128)} %bitcast.20, ...), kind=kLoop, calls=%fused_computation.9 | loop fusion | flops 15597568 | bytes 31195168 | tf_op jit(solution)/shard_map/convert_element_type | solution.py:37
  344.7 2.4 copy.5
  (10 shorter events, 2.8 us)
Async XLA Ops:
  7.2 70.2 %all-gather.5.cloned.1.call-start = ((), (), s32[]{:S(2)}) async-start(), calls=%async_computation.1 | async-start | bytes 12386304 | tf_op jit(solution)/shard_map/all_gather | solution.py:17
  7.9 191.3 %all-gather.3.cloned.1.call-start = ((), (), s32[]{:S(2)}) async-start(), calls=%async_computation | async-start | bytes 12976128 | tf_op jit(solution)/shard_map/all_gather | solution.py:18
  199.2 6.8 %copy-start = (bf16[6144,1024]{1,0:T(8,128)(2,1)S(1)}, bf16[6144,1024]{1,0:T(8,128)(2,1)}, u32[]{:S(2)}) copy-start(bf16[6144,1024]{1,0:T(8,128)(2,1)} %all-gather.3.cloned.1.call-done) | copy-start | bytes 37748740
  206.0 5.9 %copy-start.1 = (bf16[6144,896]{1,0:T(8,128)(2,1)S(1)}, bf16[6144,896]{1,0:T(8,128)(2,1)}, u32[]{:S(2)}) copy-start(bf16[6144,896]{1,0:T(8,128)(2,1)} %all-gather.5.cloned.1.call-done) | copy-start | bytes 33030148
Sparse Core Ops, SparseCore 0:
  9.8 67.4 all-gather.4
  79.9 119.2 all-gather.2
